TPU v7x, 32 devices: a whole 2x2x4 slice. The times are simulated.
32 devices in a mesh: row: 4 (over z), col: 2 (over x), depth: 4 (over y, core).
Axes of the slice: x: 2, y: 2, z: 4, core: 2. Of those that a mesh axis runs over, the one named last changes fastest.
Arguments:
- amplitudes: bfloat16 [3200, 7200], P('row', ('col', 'depth')), may hold values from -6 to 6
- integrals: bfloat16 [7200, 4096], P('row', ('col', 'depth')), may hold values from -0.0625 to 0.0625
- cycle_integrals: bfloat16 [256, 256], P('row'), as said below
- occ_irrep: int32 [100], replicated, may hold values from 0 to 7
- vir_irrep: int32 [900], replicated, may hold values from 0 to 7
Outputs:
- ladder: bfloat16 [3200, 4096], P('row', ('col', 'depth'))
- cycle: bfloat16 [256, 57600], P('row', ('col', 'depth'))
Inputs may be any that keep to these rules, and one draw needn't show every extreme that they name: cycle_integrals equals its transpose.
All inputs are finite; a program needn't handle non-finite values.
Results may differ from a plain program's by a relative error of at most 0.001.
Values may be sent and summed in bfloat16 or wider, within the bound.
A program may use at most 128 MiB of HBM per device.

v0:
```python
import jax
import jax.numpy as jnp
from jax import lax
from jax.sharding import PartitionSpec as P

NO = 100
NV = 900
JW = 64
CW = 8


def label_bits(labels):
    return jnp.stack([labels % 2, labels // 2 % 2, labels // 4 % 2])


def lookup(lookup_table, indices):
    matches = indices[:, None] == jnp.arange(lookup_table.shape[0], dtype=jnp.int32)[None, :]
    return jnp.sum(jnp.where(matches, lookup_table[None, :], 0), axis=1)


def shards(amplitudes, integrals, cycle_integrals, occ_irrep, vir_irrep):
    rows_here = amplitudes.shape[0]
    occ_block = rows_here // NO
    local_cols = amplitudes.shape[1]
    regroup_in = amplitudes.reshape(occ_block, NO, local_cols)[:, :JW, :]
    spread = lax.all_to_all(regroup_in, ("col", "depth"), split_axis=1, concat_axis=2, tiled=True)
    occ_here = spread.shape[1]
    ordered = (
        spread.reshape(occ_block, occ_here, CW, NV)
        .transpose(0, 2, 1, 3)
        .reshape(occ_block * CW, occ_here * NV)
    )
    columns = occ_here * NV
    integ_all = lax.all_gather(integrals, "row", axis=0, tiled=True)
    ladder_sum = jnp.dot(
        lax.all_gather(amplitudes, ("col", "depth"), axis=1, tiled=True),
        integ_all,
        preferred_element_type=jnp.float32,
    )
    ladder = ladder_sum.astype(jnp.bfloat16)
    cycle_rows_here = cycle_integrals.shape[0]
    cycle_sum = lax.psum_scatter(
        lax.dot_general(
            cycle_integrals, ordered, (((0,), (0,)), ((), ())), preferred_element_type=jnp.float32
        ),
        "row",
        scatter_dimension=0,
        tiled=True,
    )
    occ_bits = label_bits(occ_irrep)
    vir_bits = label_bits(vir_irrep)
    row_ids = lax.axis_index("row") * cycle_rows_here + jnp.arange(cycle_rows_here, dtype=jnp.int32)
    column_ids = lax.axis_index(("col", "depth")) * columns + jnp.arange(columns, dtype=jnp.int32)
    occ_first = row_ids // CW
    virt_first = row_ids % CW
    occ_second = column_ids // NV
    virt_second = column_ids % NV
    odd_count = jnp.zeros((cycle_rows_here, columns), jnp.int32)
    for digit in range(3):
        row_bits = lookup(occ_bits[digit], occ_first) + lookup(vir_bits[digit], virt_first)
        column_bits = lookup(occ_bits[digit], occ_second) + lookup(vir_bits[digit], virt_second)
        odd_count = odd_count + (row_bits[:, None] + column_bits[None, :]) % 2
    cycle = jnp.where(odd_count == 0, cycle_sum, jnp.float32(0.0)).astype(jnp.bfloat16)
    return (ladder, cycle)


def solution(mesh):
    in_specs = (P("row", ("col", "depth")), P("row", ("col", "depth")), P("row", None), P(), P())
    out_specs = (P("row", ("col", "depth")), P("row", ("col", "depth")))
    return jax.shard_map(shards, mesh=mesh, in_specs=in_specs, out_specs=out_specs, check_vma=False)
```

profile of v0, /device:TPU:0, one launch (start us, length us, event | category | flops | bytes accessed | tf_op | source)
XLA Modules:
  0.0 310.4 jit_solution(11669424504243657550)
XLA Ops:
  8.0 0.0 copy-start
  8.0 0.0 reduce-scatter.2.cloned.1.call-start
  8.1 3.8 %reshape.104 = bf16[8,100,900]{1,0,2:T(8,128)(2,1)S(1)} reshape(bf16[800,900]{0,1:T(8,128)(2,1)} %param.5) | data formatting | bytes 2880000 | tf_op jit(solution)/shard_map/reshape | solution.py:25
  11.8 2.8 copy.15
  14.7 19.6 %all_to_all.4 = bf16[8,64,900]{2,0,1:T(8,128)(2,1)S(1)} all-to-all(bf16[8,64,900]{2,0,1:T(8,128)(2,1)S(1)} %copy.15), channel_id=1, replica_groups=mesh['row'=4,'col'=2,'depth'=4] {'col','depth'}, dimensions={1} | all-to-all | bytes 1843200 | tf_op jit(solution)/shard_map/all_to_all | solution.py:26
  34.3 0.6 copy.16
  34.9 1.3 reshape.100
  36.2 4.2 %fusion.18 = f32[256,7200]{1,0:T(8,128)} fusion(bf16[64,256]{1,0:T(8,128)(2,1)S(1)} %copy-done, bf16[64,7200]{1,0:T(8,128)(2,1)S(1)} %reshape.100), kind=kOutput, calls=%fused_computation.91 | convolution fusion | flops 235929600 | bytes 8327168 | tf_op jit(solution)/shard_map/dot_general | solution.py:43
  40.4 0.0 reduce-scatter.2.cloned.1.call-update
  40.4 0.0 copy-start.2
  40.4 0.0 copy-start.1
  40.5 0.0 all-gather.6.cloned.1.call-start
  40.5 0.5 all-gather.6.cloned.1.call-update
  41.0 0.2 all-gather.4.cloned.1.call-start
  41.3 0.4 all-gather.4.cloned.1.call-update
  41.7 1.1 select_reduce_fusion.5
  42.9 9.3 %select_reduce_fusion.2 = (s32[7200]{0:T(1024)S(1)}, s32[7200]{0:T(1024)S(1)}, s32[7200]{0:T(1024)S(1)}) fusion(s32[900]{0:T(1024)S(1)} %get-tuple-element.16, s32[7200]{0:T(1024)S(1)} %get-tuple-element.20, s32[900]{0:T(1024)S(1)} %get-tuple-element.15, s32[900]{0:T(1024)S(1)} %get-tuple-element.14), kind=kLoop, calls=%fused_computation.2 | loop fusion | flops 45338400 | bytes 126000 | tf_op jit(solution)/shard_map/reduce_sum | solution.py:18
  52.2 0.2 select_reduce_fusion.11
  52.4 0.3 select_reduce_fusion.8
  52.8 157.8 %reduce-scatter.2.cloned.1.call-done = f32[64,7200]{1,0:T(8,128)} async-done(((f32[256,7200]{1,0:T(8,128)}), f32[64,7200]{1,0:T(8,128)}) %reduce-scatter.2.cloned.1.call-update) | async-done | bytes 1843216 | tf_op jit(solution)/shard_map/reduce_scatter | solution.py:42
  210.5 4.6 %select_convert_fusion = bf16[64,7200]{1,0:T(8,128)(2,1)} fusion(f32[64,7200]{1,0:T(8,128)} %reduce-scatter.2.cloned.1.call-done, s32[7200]{0:T(1024)S(1)} %add.222, s32[64]{0:T(128)S(1)} %add.220, s32[7200]{0:T(1024)S(1)} %add.213, s32[64]{0:T(128)S(1)} %add.211, s32[7200]{0:T(1024)S(1)} %add.205, s32[64]{0:T(128)S(1)} %add.199), kind=kLoop, calls=%fused_computation.29 | loop fusion | flops 18432000 | bytes 2851968 | tf_op jit(solution)/shard_map/convert_element_type | solution.py:63
  215.1 12.2 %reshape.103 = bf16[7200,800]{1,0:T(8,128)(2,1)} reshape(bf16[8,900,800]{2,1,0:T(8,128)(2,1)} %all-gather.6.cloned.1.call-done) | data formatting | bytes 23040000
  227.3 61.8 %all-gather.4.cloned.1.call-done = bf16[7200,512]{1,0:T(8,128)(2,1)} async-done(((bf16[1800,512]{1,0:T(8,128)(2,1)}), bf16[7200,512]{1,0:T(8,128)(2,1)}) %all-gather.4.cloned.1.call-update) | async-done | bytes 7372816 | tf_op jit(solution)/shard_map/all_gather | solution.py:34
  289.1 13.9 %convolution_convert_fusion = bf16[800,512]{1,0:T(8,128)(2,1)} fusion(bf16[7200,800]{1,0:T(8,128)(2,1)} %reshape.103, bf16[7200,512]{1,0:T(8,128)(2,1)} %all-gather.4.cloned.1.call-done), kind=kOutput, calls=%fused_computation.30 | convolution fusion | flops 5898649600 | bytes 19712000 | tf_op jit(solution)/shard_map/dot_general | solution.py:35
  (14 shorter events, 0.1 us)
Async XLA Ops:
  8.0 28.2 %copy-start = (bf16[64,256]{1,0:T(8,128)(2,1)S(1)}, bf16[64,256]{1,0:T(8,128)(2,1)}, u32[]{:S(2)}) copy-start(bf16[64,256]{1,0:T(8,128)(2,1)} %param.7) | copy-start | bytes 98308
  8.0 202.5 %reduce-scatter.2.cloned.1.call-start = ((), (), s32[]{:S(2)}) async-start(), calls=%async_computation.3 | async-start | bytes 9338880 | tf_op jit(solution)/shard_map/reduce_scatter | solution.py:42
  40.4 1.2 copy-start.2
  40.4 1.3 copy-start.1
  40.5 174.6 %all-gather.6.cloned.1.call-start = ((), (), s32[]{:S(2)}) async-start(), calls=%async_computation.4 | async-start | bytes 14579712 | tf_op jit(solution)/shard_map/all_gather | solution.py:36
  41.0 248.0 %all-gather.4.cloned.1.call-start = ((), (), s32[]{:S(2)}) async-start(), calls=%async_computation.2 | async-start | bytes 9216000 | tf_op jit(solution)/shard_map/all_gather | solution.py:34
Sparse Core Ops, SparseCore 0:
  40.5 169.9 reduce-scatter.1
Sparse Core Ops, SparseCore 1:
  42.8 73.7 all-gather.5
  118.0 171.0 all-gather.3
where the time goes:
time: 311 us; the launch traced here: 310 us
  waiting for transfers between devices  220 us (71%)
  local copies, waits for them, and re-layouts  20.7 us (7%)
  blocking collectives  19.6 us (6%)
  matrix products  18.1 us (6%)
  between operations  15.7 us (5%)
  other arithmetic  15.6 us (5%)
    reduce_scatter x1, waiting for transfers between devices, shards(): lax.psum_scatter(lax.dot_general(cycle_integrals, ordered, (((0,), (0,)),...  158 us
    all_gather x1, waiting for transfers between devices, shards(): integ_all = lax.all_gather(integrals, 'row', axis=0, tiled=True)  61.8 us
    all_to_all x1, blocking collectives, shards(): lax.all_to_all(regroup_in, ('col', 'depth'), split_axis=1, concat_axis=2,...  19.6 us
    dot_general x1, matrix products, shards(): jnp.dot(lax.all_gather(amplitudes, ('col', 'depth'), axis=1, tiled=True),...  13.9 us
    unnamed x7, local copies, waits for them, and re-layouts  12.2 us
    reduce_sum x4, other arithmetic, lookup(): return jnp.sum(jnp.where(matches, lookup_table[None, :], 0), axis=1)  10.9 us
  transfers between devices with their start and end apart: 3, of which 2 were waited for; matrix products, arithmetic and copies ran while one was open for 9% of the time, Pallas kernels for 0%

commit v1 on v0

--- a/solution.py
+++ b/solution.py
@@ -19,11 +19,23 @@
 
 
 def shards(amplitudes, integrals, cycle_integrals, occ_irrep, vir_irrep):
+
+    def reach_the_vector(slab_in, dimension_no, k_dim):
+        return jnp.concatenate(
+            jax.lax.all_to_all(
+                jnp.stack(jnp.split(slab_in, jax.lax.axis_size(("col", "depth")), dimension_no), 0),
+                ("col", "depth"),
+                0,
+                0,
+            ),
+            k_dim,
+        )
+
     rows_here = amplitudes.shape[0]
     occ_block = rows_here // NO
     local_cols = amplitudes.shape[1]
     regroup_in = amplitudes.reshape(occ_block, NO, local_cols)[:, :JW, :]
-    spread = lax.all_to_all(regroup_in, ("col", "depth"), split_axis=1, concat_axis=2, tiled=True)
+    spread = reach_the_vector(regroup_in, 1, 2)
     occ_here = spread.shape[1]
     ordered = (
         spread.reshape(occ_block, occ_here, CW, NV)

time: 311 us -> 346 us (1.11)
  local copies, waits for them, and re-layouts: 20.7 us -> 61.3 us
  waiting for transfers between devices: 220 us -> 212 us
    unnamed x3 -> x4, waiting for transfers between devices: 0.89 us -> 159 us
    reduce_scatter x1 -> x0, waiting for transfers between devices: 158 us -> none  [shards(): lax.psum_scatter(lax.dot_general(cycle_integrals, ordered, (((0,), (0,)),...]
    unnamed x7 -> x31, local copies, waits for them, and re-layouts: 12.2 us -> 49.1 us
    all_gather x1, waiting for transfers between devices: 61.8 us -> 53.6 us  [shards(): integ_all = lax.all_gather(integrals, 'row', axis=0, tiled=True)]
    split x0 -> x1, local copies, waits for them, and re-layouts: none -> 7.01 us  [reach_the_vector(): jnp.split(slab_in, jax.lax.axis_size(('col', 'depth')), dimension_no)]
  transfers between devices with their start and end apart: 3 -> 3, of which waited for: 2 -> 2; matrix products, arithmetic and copies ran while one was open for 9% -> 10% of each run, Pallas kernels for 0% -> 0%
where the time goes in v1:
time: 346 us
  waiting for transfers between devices  212 us (61%)
  local copies, waits for them, and re-layouts  61.3 us (18%)
  blocking collectives  19.6 us (6%)
  other arithmetic  18.5 us (5%)
  matrix products  18 us (5%)
  between operations  15.7 us (5%)
    unnamed x4, waiting for transfers between devices  159 us
    all_gather x1, waiting for transfers between devices, shards(): integ_all = lax.all_gather(integrals, 'row', axis=0, tiled=True)  53.6 us
    unnamed x31, local copies, waits for them, and re-layouts  49.1 us
    all_to_all x1, blocking collectives, reach_the_vector(): jax.lax.all_to_all(jnp.stack(jnp.split(slab_in, jax.lax.axis_size(('col',...  19.6 us
    dot_general x1, matrix products, shards(): jnp.dot(lax.all_gather(amplitudes, ('col', 'depth'), axis=1, tiled=True),...  13.9 us
    reduce_sum x4, other arithmetic, lookup(): return jnp.sum(jnp.where(matches, lookup_table[None, :], 0), axis=1)  10.9 us
    convert_element_type x1, other arithmetic, shards(): jnp.where(odd_count == 0, cycle_sum, jnp.float32(0.0)).astype(jnp.bfloat16)  7.5 us
    split x1, local copies, waits for them, and re-layouts, reach_the_vector(): jnp.split(slab_in, jax.lax.axis_size(('col', 'depth')), dimension_no)  7.01 us
  transfers between devices with their start and end apart: 3, of which 2 were waited for; matrix products, arithmetic and copies ran while one was open for 10% of the time, Pallas kernels for 0%

profile of v1, /device:TPU:0, one launch (start us, length us, event | category | flops | bytes accessed | tf_op | source)
XLA Modules:
  0.0 345.7 jit_solution(18019498762860151665)
XLA Ops:
  8.1 3.8 %reshape.101 = bf16[8,100,900]{1,0,2:T(8,128)(2,1)S(1)} reshape(bf16[800,900]{0,1:T(8,128)(2,1)} %param.5) | data formatting | bytes 2880000 | tf_op jit(solution)/shard_map/reshape | solution.py:37
  11.8 7.0 %fusion.18 = (bf16[8,8,900]{1,0,2:T(8,128)(2,1)}, bf16[8,8,900]{1,0,2:T(8,128)(2,1)}, bf16[8,8,900]{1,0,2:T(8,128)(2,1)}, bf16[8,8,900]{1,0,2:T(8,128)(2,1)}, bf...) fusion(bf16[8,100,900]{1,0,2:T(8,128)(2,1)S(1)} %reshape.101), kind=kLoop, calls=%fused_computation.100 | loop fusion | bytes 1843200 | tf_op jit(solution)/shard_map/split | solution.py:26
  18.9 2.6 copy.24
  21.5 3.1 copy.25
  24.6 2.3 copy.26
  26.9 3.2 copy.27
  30.1 2.5 copy.28
  32.6 2.5 copy.29
  35.1 2.5 copy.30
  37.6 1.7 copy.31
  39.2 0.9 bitcast_dynamic-update-slice_fusion.6
  42.1 19.6 %all_to_all.5 = bf16[8,8,8,900]{3,2,1,0:T(8,128)(2,1)S(1)} all-to-all(bf16[8,8,8,900]{3,2,1,0:T(8,128)(2,1)S(1)} %bitcast_dynamic-update-slice_fusion), channel_id=1, replica_groups=mesh['row'=4,'col'=2,'depth'=4] {'col','depth'}, dimensions={0} | all-to-all | bytes 1843200 | tf_op jit(solution)/shard_map/all_to_all | solution.py:25
  61.8 1.3 reshape.97
  63.1 4.1 %convolution_bitcast_fusion = f32[256,7200]{0,1:T(8,128)} fusion(bf16[64,7200]{1,0:T(8,128)(2,1)S(1)} %reshape.97, bf16[64,256]{1,0:T(8,128)(2,1)S(1)} %copy-done), kind=kOutput, calls=%fused_computation.4 | convolution fusion | flops 235929600 | bytes 8327168 | tf_op jit(solution)/shard_map/dot_general | solution.py:55
  67.2 8.5 %copy.22 = f32[256,7200]{1,0:T(8,128)} copy(f32[256,7200]{0,1:T(8,128)} %convolution_bitcast_fusion) | data formatting | bytes 14745600
  77.0 1.1 select_reduce_fusion.5
  78.1 9.3 %select_reduce_fusion.2 = (s32[7200]{0:T(1024)S(1)}, s32[7200]{0:T(1024)S(1)}, s32[7200]{0:T(1024)S(1)}) fusion(s32[900]{0:T(1024)S(1)} %get-tuple-element.32, s32[7200]{0:T(1024)S(1)} %get-tuple-element.36, s32[900]{0:T(1024)S(1)} %get-tuple-element.31, s32[900]{0:T(1024)S(1)} %get-tuple-element.30), kind=kLoop, calls=%fused_computation.2 | loop fusion | flops 45338400 | bytes 126000 | tf_op jit(solution)/shard_map/reduce_sum | solution.py:18
  88.0 157.8 %reduce-scatter.4.cloned.1.call-done = f32[64,7200]{1,0:T(8,128)} async-done(((f32[256,7200]{1,0:T(8,128)}), f32[64,7200]{1,0:T(8,128)}) %reduce-scatter.4.cloned.1.call-update) | async-done | bytes 1843216
  245.8 2.6 copy.23
  248.5 7.5 %select_convert_fusion = bf16[64,7200]{0,1:T(8,128)(2,1)} fusion(bf16[64,7200]{0,1:T(8,128)(2,1)S(1)} %copy.23, s32[7200]{0:T(1024)S(1)} %add.222, s32[64]{0:T(128)S(1)} %add.220, s32[7200]{0:T(1024)S(1)} %add.213, s32[64]{0:T(128)S(1)} %add.211, s32[7200]{0:T(1024)S(1)} %add.205, s32[64]{0:T(128)S(1)} %add.199), kind=kLoop, calls=%fused_computation.26 | loop fusion | flops 18432000 | bytes 1930368 | tf_op jit(solution)/shard_map/convert_element_type | solution.py:75
  256.0 2.6 copy.19
  258.6 12.2 %reshape.100 = bf16[7200,800]{1,0:T(8,128)(2,1)} reshape(bf16[8,900,800]{2,1,0:T(8,128)(2,1)} %all-gather.6.cloned.1.call-done) | data formatting | bytes 23040000
  270.8 53.6 %all-gather.4.cloned.1.call-done = bf16[7200,512]{1,0:T(8,128)(2,1)} async-done(((bf16[1800,512]{1,0:T(8,128)(2,1)}), bf16[7200,512]{1,0:T(8,128)(2,1)}) %all-gather.4.cloned.1.call-update) | async-done | bytes 7372816 | tf_op jit(solution)/shard_map/all_gather | solution.py:46
  324.4 13.9 %convolution_convert_fusion = bf16[800,512]{1,0:T(8,128)(2,1)} fusion(bf16[7200,800]{1,0:T(8,128)(2,1)} %reshape.100, bf16[7200,512]{1,0:T(8,128)(2,1)} %all-gather.4.cloned.1.call-done), kind=kOutput, calls=%fused_computation.31 | convolution fusion | flops 5898649600 | bytes 19712000 | tf_op jit(solution)/shard_map/dot_general | solution.py:47
  (39 shorter events, 3.8 us)
Async XLA Ops:
  8.0 55.1 %copy-start = (bf16[64,256]{1,0:T(8,128)(2,1)S(1)}, bf16[64,256]{1,0:T(8,128)(2,1)}, u32[]{:S(2)}) copy-start(bf16[64,256]{1,0:T(8,128)(2,1)} %param.7) | copy-start | bytes 98308
  8.0 237.8 %reduce-scatter.4.cloned.1.call-start = ((), (), s32[]{:S(2)}) async-start(), calls=%async_computation.4 | async-start | bytes 9338880
  18.9 5.7 %copy-start.3 = (bf16[8,8,900]{1,0,2:T(8,128)(2,1)S(1)}, bf16[8,8,900]{1,0,2:T(8,128)(2,1)}, u32[]{:S(2)}) copy-start(bf16[8,8,900]{1,0,2:T(8,128)(2,1)} %get-tuple-element.27) | copy-start | bytes 345604
  26.9 10.7 %copy-start.2 = (bf16[8,8,900]{1,0,2:T(8,128)(2,1)S(1)}, bf16[8,8,900]{1,0,2:T(8,128)(2,1)}, u32[]{:S(2)}) copy-start(bf16[8,8,900]{1,0,2:T(8,128)(2,1)} %get-tuple-element.22) | copy-start | bytes 345604
  75.7 1.3 copy-start.5
  75.7 1.3 copy-start.4
  75.7 182.9 %all-gather.6.cloned.1.call-start = ((), (), s32[]{:S(2)}) async-start(), calls=%async_computation.3 | async-start | bytes 14579712 | tf_op jit(solution)/shard_map/all_gather | solution.py:48
  76.3 248.0 %all-gather.4.cloned.1.call-start = ((), (), s32[]{:S(2)}) async-start(), calls=%async_computation.2 | async-start | bytes 9216000 | tf_op jit(solution)/shard_map/all_gather | solution.py:46
  324.4 13.9 %copy-start.1 = (bf16[64,256]{1,0:T(8,128)(2,1)S(1)}, bf16[64,256]{1,0:T(8,128)(2,1)}, u32[]{:S(2)}) copy-start(bf16[64,256]{1,0:T(8,128)(2,1)} %param.7) | copy-start | bytes 98308
Sparse Core Ops, SparseCore 0:
  75.9 169.9 reduce-scatter.3
Sparse Core Ops, SparseCore 1:
  78.1 73.7 all-gather.5
  153.3 171.0 all-gather.3
